TPU v7x, 32 devices: a whole 2x2x4 slice. The times are simulated.
32 devices in a mesh: dp: 8 (over z, x), ctx: 4 (over y, core).
Axes of the slice: x: 2, y: 2, z: 4, core: 2. Of those that a mesh axis runs over, the one named last changes fastest.
Arguments:
- inputs: bfloat16 [512, 16, 1024], P('ctx', 'dp'), may hold values from -6 to 6
- cotangent: bfloat16 [512, 16, 1024], P('ctx', 'dp'), may hold values from -6 to 6
- lengths: int32 [16], P('dp'), may hold values from 128 to 512, as said below
- block_order: int32 [8], replicated, may hold values from 0 to 7, as said below
- norm_gain: bfloat16 [1024], P('dp'), may hold values from 0.5 to 1.5
- norm_bias: bfloat16 [1024], P('dp'), may hold values from -1.75 to 1.75
- attend_weight: bfloat16 [1024, 3072], P('dp'), may hold values from -0.1875 to 0.1875
- attend_bias: bfloat16 [3072], P('dp'), may hold values from -3 to 3
- dense_weight: bfloat16 [1024, 1024], P('dp'), may hold values from -6 to 6
- dense_bias: bfloat16 [1024], P('dp'), may hold values from -3 to 3
- up_weight: bfloat16 [1024, 4096], P('dp'), may hold values from -0.1875 to 0.1875
- up_bias: bfloat16 [4096], P('dp'), may hold values from -3 to 3
- down_weight: bfloat16 [4096, 1024], P('dp'), may hold values from -0.09375 to 0.09375
- down_bias: bfloat16 [1024], P('dp'), may hold values from -3 to 3
Outputs:
- output: bfloat16 [512, 16, 1024], P('ctx', 'dp')
- input_grad: bfloat16 [512, 16, 1024], P('ctx', 'dp')
- grad_norm_gain: float32 [1024], P('dp')
- grad_norm_bias: float32 [1024], P('dp')
- grad_attend_weight: float32 [1024, 3072], P('dp')
- grad_attend_bias: float32 [3072], P('dp')
- grad_dense_weight: float32 [1024, 1024], P('dp')
- grad_dense_bias: float32 [1024], P('dp')
- grad_up_weight: float32 [1024, 4096], P('dp')
- grad_up_bias: float32 [4096], P('dp')
- grad_down_weight: float32 [4096, 1024], P('dp')
- grad_down_bias: float32 [1024], P('dp')
Inputs may be any that keep to these rules, and one draw needn't show every extreme that they name: Slots of sequence s whose position is lengths[s] or more are padding; in every draw some sequence has exactly 512 valid slots and some exactly 128. Each of 0 to 7 appears once, and block_order[2 c] + block_order[2 c + 1] = 7 for every c.
All inputs are finite; a program needn't handle non-finite values.
Results may differ from a plain program's by a relative error of at most 0.018.
Values may be sent and summed in bfloat16 or wider, within the bound.
No kernel may reach another device: no remote copies, remote signals or barrier semaphores. Data moves between devices by JAX's collectives and lax.ppermute only.
A program may use at most 320 MiB of HBM per device.

v0:
```python
import math
import jax
import jax.numpy as jnp
from jax import lax
from jax.sharding import PartitionSpec as P

HEADS = 16
HEAD_DIM = 64
ROT = 16
BLK = 64
EPSILON = 1e-05
ROOT_HALF = 0.7071067811865476
NORMAL_PEAK = 0.3989422804014327


def place_of(block_order, first_slot, count):
    slot = first_slot + jnp.arange(count, dtype=jnp.int32)
    which = slot // BLK
    table = jnp.arange(block_order.shape[0], dtype=jnp.int32)
    chosen = jnp.sum(jnp.where(which[:, None] == table[None, :], block_order[None, :], 0), axis=1)
    return chosen * BLK + slot % BLK


def angles(places):
    rates = 10000.0 ** (-jnp.arange(0, ROT, 2, dtype=jnp.float32) / ROT)
    turned = places.astype(jnp.float32)[:, None] * rates[None, :]
    doubled = jnp.concatenate([turned, turned], axis=-1)
    return (jnp.cos(doubled), jnp.sin(doubled))


def turn_half(values):
    half = values.shape[-1] // 2
    return jnp.concatenate([-values[..., half:], values[..., :half]], axis=-1)


def rotary(values, cosine, sine):
    front = values[..., :ROT]
    moved = front * cosine[:, None, None, :] + turn_half(front) * sine[:, None, None, :]
    return jnp.concatenate([moved, values[..., ROT:]], axis=-1)


def sweep(step_fn, carry, piece, start):
    count = jax.tree.leaves(piece)[0].shape[0]
    size = math.gcd(count, 512)
    if size == count:
        return step_fn(carry, piece, start)

    def inner(turn, state):
        part = jax.tree.map(
            lambda array: lax.dynamic_slice_in_dim(array, turn * size, size, 0), piece
        )
        return step_fn(state, part, start + turn * size)

    return lax.fori_loop(0, count // size, inner, carry)


def body(
    inputs,
    cotangent,
    lengths,
    block_order,
    norm_gain,
    norm_bias,
    attend_weight,
    attend_bias,
    dense_weight,
    dense_bias,
    up_weight,
    up_bias,
    down_weight,
    down_bias,
):
    local, sequences, width = inputs.shape
    rows = local * sequences
    scale = HEAD_DIM ** (-0.5)
    first_slot = lax.axis_index("ctx") * local
    places = place_of(block_order, first_slot, local)
    valid = (places[:, None] < lengths[None, :]).astype(jnp.float32)
    (
        gain,
        shift,
        attend_full,
        attend_shift,
        dense_full,
        dense_shift,
        up_full,
        up_shift,
        down_full,
        down_shift,
    ) = (
        lax.all_gather(norm_gain, "dp", axis=0, tiled=True),
        lax.all_gather(norm_bias, "dp", axis=0, tiled=True),
        lax.all_gather(attend_weight, "dp", axis=0, tiled=True),
        lax.all_gather(attend_bias, "dp", axis=0, tiled=True),
        lax.all_gather(dense_weight, "dp", axis=0, tiled=True),
        lax.all_gather(dense_bias, "dp", axis=0, tiled=True),
        lax.all_gather(up_weight, "dp", axis=0, tiled=True),
        lax.all_gather(up_bias, "dp", axis=0, tiled=True),
        lax.all_gather(down_weight, "dp", axis=0, tiled=True),
        lax.all_gather(down_bias, "dp", axis=0, tiled=True),
    )
    source = inputs.astype(jnp.float32)
    mean = jnp.mean(source, axis=-1, keepdims=True)
    centred = source - mean
    inverse = lax.rsqrt(jnp.mean(centred * centred, axis=-1, keepdims=True) + EPSILON)
    unit = centred * inverse
    normed_low = (
        (unit * gain.astype(jnp.float32) + shift.astype(jnp.float32))
        .astype(jnp.bfloat16)
        .reshape(rows, width)
    )
    projected = (
        jnp.dot(normed_low, attend_full, preferred_element_type=jnp.float32)
        + attend_shift.astype(jnp.float32)
    ).reshape(local, sequences, 3, HEADS, HEAD_DIM)
    cosine, sine = angles(places)
    queries = rotary(projected[:, :, 0], cosine, sine).astype(jnp.bfloat16)
    key_rot = rotary(projected[:, :, 1], cosine, sine).astype(jnp.bfloat16)
    value_low = projected[:, :, 2].astype(jnp.bfloat16)
    key_pairs = jnp.concatenate(
        [key_rot.reshape(local, sequences, width), value_low.reshape(local, sequences, width)],
        axis=-1,
    )

    def split_pairs(piece):
        count = piece.shape[0]
        return (
            piece[..., :width].reshape(count, sequences, HEADS, HEAD_DIM),
            piece[..., width:].reshape(count, sequences, HEADS, HEAD_DIM),
        )

    def exp_weights(piece, start):
        key_part, value_part = split_pairs(piece)
        key_places = place_of(block_order, start, piece.shape[0])
        scores = (
            jnp.einsum("qshd,kshd->shqk", queries, key_part, preferred_element_type=jnp.float32)
            * scale
        )
        allowed = key_places[None, :] <= places[:, None]
        return (jnp.where(allowed, jnp.exp(scores), 0.0), key_part, value_part)

    def forward_step(carry, piece, start):
        summed, total = carry
        weights, key_part, value_part = exp_weights(piece, start)
        summed = summed + jnp.einsum(
            "shqk,kshd->shqd",
            weights.astype(jnp.bfloat16),
            value_part,
            preferred_element_type=jnp.float32,
        )
        return (summed, total + jnp.sum(weights, axis=-1))

    start_carry = (
        jnp.zeros((sequences, HEADS, local, HEAD_DIM), jnp.float32),
        jnp.zeros((sequences, HEADS, local), jnp.float32),
    )
    summed, total = sweep(
        forward_step,
        start_carry,
        lax.all_gather(key_pairs, "ctx", axis=0, tiled=True),
        jnp.int32(0),
    )
    mixed = summed / total[..., None]
    mixed_low = jnp.transpose(mixed, (2, 0, 1, 3)).reshape(rows, width).astype(jnp.bfloat16)
    hidden = jnp.dot(normed_low, up_full, preferred_element_type=jnp.float32) + up_shift.astype(
        jnp.float32
    )
    active_low = jax.nn.gelu(hidden, approximate=False).astype(jnp.bfloat16)
    branch = (
        jnp.dot(mixed_low, dense_full, preferred_element_type=jnp.float32)
        + dense_shift.astype(jnp.float32)
        + jnp.dot(active_low, down_full, preferred_element_type=jnp.float32)
        + down_shift.astype(jnp.float32)
    )
    output = (valid[..., None] * (source + branch.reshape(local, sequences, width))).astype(
        jnp.bfloat16
    )
    pulled = valid[..., None] * cotangent.astype(jnp.float32)
    pulled_low = pulled.astype(jnp.bfloat16).reshape(rows, width)
    bias_grad = jnp.sum(pulled_low.astype(jnp.float32), axis=0)
    grad_dense = jnp.dot(mixed_low.T, pulled_low, preferred_element_type=jnp.float32)
    grad_down = jnp.dot(active_low.T, pulled_low, preferred_element_type=jnp.float32)
    slope = (
        0.5 * (1.0 + lax.erf(hidden * ROOT_HALF))
        + hidden * jnp.exp(-0.5 * hidden * hidden) * NORMAL_PEAK
    )
    back_hidden_low = (
        jnp.dot(pulled_low, down_full.T, preferred_element_type=jnp.float32) * slope
    ).astype(jnp.bfloat16)
    grad_up_shift = jnp.sum(back_hidden_low.astype(jnp.float32), axis=0)
    grad_up = jnp.dot(normed_low.T, back_hidden_low, preferred_element_type=jnp.float32)
    back_mixed = jnp.transpose(
        jnp.dot(pulled_low, dense_full.T, preferred_element_type=jnp.float32).reshape(
            local, sequences, HEADS, HEAD_DIM
        ),
        (1, 2, 0, 3),
    )
    scaled_low = (back_mixed / total[..., None]).astype(jnp.bfloat16)
    correction = jnp.sum(back_mixed * mixed, axis=-1) / total
    ready_pairs = lax.all_gather(key_pairs, "ctx", axis=0, tiled=True)

    def slopes_of(piece, start):
        weights, key_part, value_part = exp_weights(piece, start)
        pressure = jnp.einsum(
            "shqd,kshd->shqk", scaled_low, value_part, preferred_element_type=jnp.float32
        )
        slopes_low = (weights * (pressure - correction[..., None])).astype(jnp.bfloat16)
        return (weights, slopes_low, key_part)

    def query_step(carry, piece, start):
        weights, slopes_low, key_part = slopes_of(piece, start)
        return (
            carry
            + jnp.einsum(
                "shqk,kshd->shqd", slopes_low, key_part, preferred_element_type=jnp.float32
            )
            * scale
        )

    back_queries = sweep(
        query_step, jnp.zeros((sequences, HEADS, local, HEAD_DIM), jnp.float32), ready_pairs, 0
    )

    def key_block(start, size):
        piece = lax.dynamic_slice_in_dim(ready_pairs, start, size, 0)
        weights, slopes_low, key_part = slopes_of(piece, start)
        back_keys = (
            jnp.einsum("shqk,qshd->kshd", slopes_low, queries, preferred_element_type=jnp.float32)
            * scale
        )
        back_values = jnp.einsum(
            "shqk,shqd->kshd",
            weights.astype(jnp.bfloat16),
            scaled_low,
            preferred_element_type=jnp.float32,
        )
        return jnp.concatenate(
            [
                back_keys.reshape(size, sequences, width),
                back_values.reshape(size, sequences, width),
            ],
            axis=-1,
        )

    def key_terms(start, count):
        size = math.gcd(count, 512)
        if size == count:
            return key_block(start, count)

        def one_block(turn):
            return key_block(start + turn * size, size)

        blocks = lax.map(one_block, jnp.arange(count // size, dtype=jnp.int32))
        return blocks.reshape(count, sequences, 2 * width)

    pair_grads = lax.psum_scatter(
        key_terms(jnp.int32(0), local * lax.axis_size("ctx")).astype(jnp.bfloat16),
        "ctx",
        scatter_dimension=0,
        tiled=True,
    ).astype(jnp.float32)
    back_key_rows = pair_grads[..., :width].reshape(local, sequences, HEADS, HEAD_DIM)
    back_value_rows = pair_grads[..., width:].reshape(local, sequences, HEADS, HEAD_DIM)
    back_query_rows = jnp.transpose(back_queries, (2, 0, 1, 3))
    back_projected_low = (
        jnp.stack(
            [
                rotary(back_query_rows, cosine, -sine),
                rotary(back_key_rows, cosine, -sine),
                back_value_rows,
            ],
            axis=2,
        )
        .reshape(rows, 3 * width)
        .astype(jnp.bfloat16)
    )
    grad_attend_shift = jnp.sum(back_projected_low.astype(jnp.float32), axis=0)
    grad_attend = jnp.dot(normed_low.T, back_projected_low, preferred_element_type=jnp.float32)
    back_normed = (
        jnp.dot(back_projected_low, attend_full.T, preferred_element_type=jnp.float32)
        + jnp.dot(back_hidden_low, up_full.T, preferred_element_type=jnp.float32)
    ).reshape(local, sequences, width)
    grad_gain = jnp.sum(back_normed * unit, axis=(0, 1))
    grad_shift = jnp.sum(back_normed, axis=(0, 1))
    back_unit = back_normed * gain.astype(jnp.float32)
    back_source = inverse * (
        back_unit
        - jnp.mean(back_unit, axis=-1, keepdims=True)
        - unit * jnp.mean(back_unit * unit, axis=-1, keepdims=True)
    )
    input_grad = (pulled + back_source).astype(jnp.bfloat16)
    terms = (
        grad_gain,
        grad_shift,
        grad_attend,
        grad_attend_shift,
        grad_dense,
        bias_grad,
        grad_up,
        grad_up_shift,
        grad_down,
        bias_grad,
    )
    shards = (
        lax.psum_scatter(
            terms[0].astype(jnp.bfloat16), "dp", scatter_dimension=0, tiled=True
        ).astype(jnp.float32),
        lax.psum_scatter(
            terms[1].astype(jnp.bfloat16), "dp", scatter_dimension=0, tiled=True
        ).astype(jnp.float32),
        lax.psum_scatter(
            terms[2].astype(jnp.bfloat16), "dp", scatter_dimension=0, tiled=True
        ).astype(jnp.float32),
        lax.psum_scatter(
            terms[3].astype(jnp.bfloat16), "dp", scatter_dimension=0, tiled=True
        ).astype(jnp.float32),
        lax.psum_scatter(
            terms[4].astype(jnp.bfloat16), "dp", scatter_dimension=0, tiled=True
        ).astype(jnp.float32),
        lax.psum_scatter(
            terms[5].astype(jnp.bfloat16), "dp", scatter_dimension=0, tiled=True
        ).astype(jnp.float32),
        lax.psum_scatter(
            terms[6].astype(jnp.bfloat16), "dp", scatter_dimension=0, tiled=True
        ).astype(jnp.float32),
        lax.psum_scatter(
            terms[7].astype(jnp.bfloat16), "dp", scatter_dimension=0, tiled=True
        ).astype(jnp.float32),
        lax.psum_scatter(
            terms[8].astype(jnp.bfloat16), "dp", scatter_dimension=0, tiled=True
        ).astype(jnp.float32),
        lax.psum_scatter(
            terms[9].astype(jnp.bfloat16), "dp", scatter_dimension=0, tiled=True
        ).astype(jnp.float32),
    )
    reduced = (
        lax.psum(shards[0].astype(jnp.bfloat16), "ctx").astype(jnp.float32),
        lax.psum(shards[1].astype(jnp.bfloat16), "ctx").astype(jnp.float32),
        lax.psum(shards[2].astype(jnp.bfloat16), "ctx").astype(jnp.float32),
        lax.psum(shards[3].astype(jnp.bfloat16), "ctx").astype(jnp.float32),
        lax.psum(shards[4].astype(jnp.bfloat16), "ctx").astype(jnp.float32),
        lax.psum(shards[5].astype(jnp.bfloat16), "ctx").astype(jnp.float32),
        lax.psum(shards[6].astype(jnp.bfloat16), "ctx").astype(jnp.float32),
        lax.psum(shards[7].astype(jnp.bfloat16), "ctx").astype(jnp.float32),
        lax.psum(shards[8].astype(jnp.bfloat16), "ctx").astype(jnp.float32),
        lax.psum(shards[9].astype(jnp.bfloat16), "ctx").astype(jnp.float32),
    )
    return (
        output,
        input_grad,
        reduced[0],
        reduced[1],
        reduced[2],
        reduced[3],
        reduced[4],
        reduced[5],
        reduced[6],
        reduced[7],
        reduced[8],
        reduced[9],
    )


def solution(mesh):
    return jax.shard_map(
        body,
        mesh=mesh,
        in_specs=(
            P("ctx", "dp", None),
            P("ctx", "dp", None),
            P("dp"),
            P(),
            P("dp"),
            P("dp"),
            P("dp", None),
            P("dp"),
            P("dp", None),
            P("dp"),
            P("dp", None),
            P("dp"),
            P("dp", None),
            P("dp"),
        ),
        out_specs=(
            P("ctx", "dp", None),
            P("ctx", "dp", None),
            P("dp"),
            P("dp"),
            P("dp", None),
            P("dp"),
            P("dp", None),
            P("dp"),
            P("dp", None),
            P("dp"),
            P("dp", None),
            P("dp"),
        ),
        check_vma=False,
    )
```

profile of v0, /device:TPU:0, one launch (start us, length us, event | category | flops | bytes accessed | tf_op | source)
XLA Modules:
  0.0 1102.6 jit_solution(300780800760500734)
XLA Ops:
  8.7 22.8 %all-gather = bf16[8,1,128]{2,1,0:T(2,128)(2,1)S(1)} all-gather(bf16[1,1,128]{2,1,0:T(2,128)(2,1)} %bitcast.110), channel_id=1, replica_groups=mesh['dp'=8,'ctx'=4] {'dp'}, dimensions={0}, use_global_device_ids=true | all-gather | bytes 2304 | tf_op jit(solution)/shard_map/all_gather | solution.py:91
  31.5 17.2 %all-gather.1 = bf16[8,1,128]{2,1,0:T(2,128)(2,1)S(1)} all-gather(bf16[1,1,128]{2,1,0:T(2,128)(2,1)} %bitcast.111), channel_id=1, replica_groups=mesh['dp'=8,'ctx'=4] {'dp'}, dimensions={0}, use_global_device_ids=true | all-gather | bytes 2304 | tf_op jit(solution)/shard_map/all_gather | solution.py:92
  48.7 27.0 %all-gather.2 = bf16[8,1,384]{2,1,0:T(2,128)(2,1)S(1)} all-gather(bf16[1,1,384]{2,1,0:T(2,128)(2,1)S(1)} %reshape.296), channel_id=1, replica_groups=mesh['dp'=8,'ctx'=4] {'dp'}, dimensions={0}, use_global_device_ids=true | all-gather | bytes 6912 | tf_op jit(solution)/shard_map/all_gather | solution.py:94
  82.2 29.6 %all-gather.12.cloned.1.call-done = bf16[1024,3072]{1,0:T(8,128)(2,1)} async-done(((bf16[128,3072]{1,0:T(8,128)(2,1)}), bf16[1024,3072]{1,0:T(8,128)(2,1)}) %all-gather.12.cloned.1.call-update) | async-done | bytes 6291472 | tf_op jit(solution)/shard_map/all_gather | solution.py:93
  111.8 6.3 convolution_add_fusion.1
  149.0 27.8 %all-gather.14.cloned.1.call-done = bf16[512,2,2048]{0,2,1:T(8,128)(2,1)} async-done(((bf16[128,2,2048]{0,2,1:T(8,128)(2,1)}), bf16[512,2,2048]{0,2,1:T(8,128)(2,1)}) %all-gather.14.cloned.1.call-update) | async-done | bytes 4194320 | tf_op jit(solution)/shard_map/all_gather | solution.py:160
  187.7 40.4 %all-gather.16.cloned.1.call-done = bf16[1024,1024]{1,0:T(8,128)(2,1)} async-done(((bf16[128,1024]{1,0:T(8,128)(2,1)}), bf16[1024,1024]{1,0:T(8,128)(2,1)}) %all-gather.16.cloned.1.call-update) | async-done | bytes 2097168 | tf_op jit(solution)/shard_map/all_gather | solution.py:95
  240.7 6.4 copy.60
  257.8 26.8 %all-gather.4 = bf16[8,1,512]{2,1,0:T(2,128)(2,1)S(1)} all-gather(bf16[1,1,512]{2,1,0:T(2,128)(2,1)S(1)} %reshape.300), channel_id=1, replica_groups=mesh['dp'=8,'ctx'=4] {'dp'}, dimensions={0}, use_global_device_ids=true | all-gather | bytes 9216 | tf_op jit(solution)/shard_map/all_gather | solution.py:98
  284.7 68.7 %all-gather.18.cloned.1.call-done = bf16[1024,4096]{1,0:T(8,128)(2,1)} async-done(((bf16[128,4096]{1,0:T(8,128)(2,1)}), bf16[1024,4096]{1,0:T(8,128)(2,1)}) %all-gather.18.cloned.1.call-update) | async-done | bytes 8388624 | tf_op jit(solution)/shard_map/all_gather | solution.py:97
  353.3 14.5 %fusion.5 = (bf16[256,4096]{1,0:T(8,128)(2,1)S(1)}, f32[256,4096]{1,0:T(8,128)}) fusion(f32[4096]{0:T(1024)S(1)} %bitcast.106, bf16[256,1024]{1,0:T(8,128)(2,1)S(1)} %reshape.282, bf16[1024,4096]{1,0:T(8,128)(2,1)} %all-gather.18.cloned.1.call-done), kind=kOutput, calls=%fused_computation.14 | convolution fusion | flops 2216689664 | bytes 15220736 | tf_op jit(solution)/shard_map/dot_general | solution.py:165
  375.3 102.6 %all-gather.20.cloned.1.call-done = bf16[4096,1024]{1,0:T(8,128)(2,1)} async-done(((bf16[512,1024]{1,0:T(8,128)(2,1)}), bf16[4096,1024]{1,0:T(8,128)(2,1)}) %all-gather.20.cloned.1.call-update) | async-done | bytes 8388624 | tf_op jit(solution)/shard_map/all_gather | solution.py:99
  477.9 6.5 fusion.64
  496.7 26.4 %reduce-scatter.16.cloned.1.call-done = bf16[128,4096]{1,0:T(8,128)(2,1)} async-done(((bf16[512,4096]{1,0:T(8,128)(2,1)}), bf16[128,4096]{1,0:T(8,128)(2,1)}) %reduce-scatter.16.cloned.1.call-update) | async-done | bytes 1048592
  536.0 6.0 convolution_convert_fusion.2
  545.1 20.5 %all-gather.3 = bf16[8,1,128]{2,1,0:T(2,128)(2,1)S(1)} all-gather(bf16[1,1,128]{2,1,0:T(2,128)(2,1)S(1)} %bitcast.112), channel_id=1, replica_groups=mesh['dp'=8,'ctx'=4] {'dp'}, dimensions={0}, use_global_device_ids=true | all-gather | bytes 2304 | tf_op jit(solution)/shard_map/all_gather | solution.py:96
  565.6 16.4 %all-gather.5 = bf16[8,1,128]{2,1,0:T(2,128)(2,1)S(1)} all-gather(bf16[1,1,128]{2,1,0:T(2,128)(2,1)S(1)} %bitcast.113), channel_id=1, replica_groups=mesh['dp'=8,'ctx'=4] {'dp'}, dimensions={0}, use_global_device_ids=true | all-gather | bytes 2304 | tf_op jit(solution)/shard_map/all_gather | solution.py:100
  588.0 6.9 fusion.66
  598.5 146.8 %reduce-scatter.14.cloned.1.call-done = bf16[512,1024]{1,0:T(8,128)(2,1)} async-done(((bf16[4096,1024]{1,0:T(8,128)(2,1)}), bf16[512,1024]{1,0:T(8,128)(2,1)}) %reduce-scatter.14.cloned.1.call-update) | async-done | bytes 1048592 | tf_op jit(solution)/shard_map/reduce_scatter | solution.py:329
  745.4 150.3 %reduce-scatter.12.cloned.1.call-done = bf16[128,4096]{1,0:T(8,128)(2,1)} async-done(((bf16[1024,4096]{1,0:T(8,128)(2,1)}), bf16[128,4096]{1,0:T(8,128)(2,1)}) %reduce-scatter.12.cloned.1.call-update) | async-done | bytes 1048592 | tf_op jit(solution)/shard_map/reduce_scatter | solution.py:323
  895.6 120.6 %reduce-scatter.8.cloned.1.call-done = bf16[128,3072]{1,0:T(8,128)(2,1)} async-done(((bf16[1024,3072]{1,0:T(8,128)(2,1)}), bf16[128,3072]{1,0:T(8,128)(2,1)}) %reduce-scatter.8.cloned.1.call-update) | async-done | bytes 786448 | tf_op jit(solution)/shard_map/reduce_scatter | solution.py:311
  1026.1 35.3 %all-reduce.5 = (bf16[1024]{0:T(1024)(128)(2,1)S(1)}, bf16[1024]{0:T(1024)(128)(2,1)S(1)}, bf16[3072]{0:T(1024)(128)(2,1)S(1)}, bf16[1024]{0:T(1024)(128)(2,1)S(1)}, bf16[4096]{0:T(1024)(128)(2,1)S(1)}) all-reduce(bf16[1024]{0:T(1024)(128)(2,1)S(1)} %get-tuple-element.12, ...), channel_id=3, replica_groups=mesh['dp'=8,'ctx'=4] {'dp'}, use_global_device_ids=true, to_apply=%region_10.11.clone | all-reduce | flops 10240 | bytes 40960
  1061.8 6.5 all-reduce.6
  1073.7 13.0 %all-reduce.10.cloned.1.call-done = (bf16[128,3072]{1,0:T(8,128)(2,1)}, bf16[128,1024]{1,0:T(8,128)(2,1)}, bf16[128,4096]{1,0:T(8,128)(2,1)}, bf16[512,1024]{1,0:T(8,128)(2,1)}) async-done(((bf16[128,3072]{1,0:T(8,128)(2,1)}, bf16[128,1024]{1,0:T(8,128)(2,1)}, bf16[128,4096]{1,0:T(8,128)(2,1)}, bf16[512,1024]{1,0:T(8,128)(2,1)}), (bf16[128,3072]{1,0:T(8,128)(2,1)}, bf16[128,1024]{1,0:T(8,128)(2,1)}, ...) | async-done | bytes 3145744 | tf_op jit(solution)/shard_map/psum | solution.py:339
  (185 shorter events, 140.5 us)
Async XLA Ops:
  7.2 74.2 %copy-start.23 = (s32[8]{0:T(128)S(1)}, s32[8]{0:T(128)}, u32[]{:S(2)}) copy-start(s32[8]{0:T(128)} %param.17) | copy-start | bytes 100
  7.2 104.6 %all-gather.12.cloned.1.call-start = ((), (), s32[]{:S(2)}) async-start(), calls=%async_computation.5 | async-start | bytes 7077888 | tf_op jit(solution)/shard_map/all_gather | solution.py:93
  7.9 168.9 %all-gather.14.cloned.1.call-start = ((), (), s32[]{:S(2)}) async-start(), calls=%async_computation.6 | async-start | bytes 5242880 | tf_op jit(solution)/shard_map/all_gather | solution.py:160
  81.3 403.2 %copy-start.3 = (bf16[256,1024]{1,0:T(8,128)(2,1)}, bf16[256,1024]{1,0:T(8,128)(2,1)S(1)}, u32[]{:S(2)}) copy-start(bf16[256,1024]{1,0:T(8,128)(2,1)S(1)} %reshape.282) | copy-start | bytes 1572868
  143.5 84.6 %all-gather.16.cloned.1.call-start = ((), (), s32[]{:S(2)}) async-start(), calls=%async_computation.7 | async-start | bytes 2359296 | tf_op jit(solution)/shard_map/all_gather | solution.py:95
  144.2 209.1 %all-gather.18.cloned.1.call-start = ((), (), s32[]{:S(2)}) async-start(), calls=%async_computation.8 | async-start | bytes 9437184 | tf_op jit(solution)/shard_map/all_gather | solution.py:97
  144.8 333.2 %all-gather.20.cloned.1.call-start = ((), (), s32[]{:S(2)}) async-start(), calls=%async_computation.9 | async-start | bytes 9437184 | tf_op jit(solution)/shard_map/all_gather | solution.py:99
  145.4 377.8 %reduce-scatter.16.cloned.1.call-start = ((), (), s32[]{:S(2)}) async-start(), calls=%async_computation.14 | async-start | bytes 5242880
  146.8 81.3 %copy-start.9 = (bf16[128,2,1024]{2,1,0:T(2,128)(2,1)}, bf16[128,2,1024]{2,1,0:T(2,128)(2,1)S(1)}, u32[]{:S(2)}) copy-start(bf16[128,2,1024]{2,1,0:T(2,128)(2,1)S(1)} %get-tuple-element.31) | copy-start | bytes 1572868
  228.1 8.7 slice-start
  247.1 351.4 %reduce-scatter.10.cloned.1.call-start = ((), (), s32[]{:S(2)}) async-start(), calls=%async_computation.11 | async-start | bytes 2359296 | tf_op jit(solution)/shard_map/reduce_scatter | solution.py:317
  248.7 9.1 copy-start.22
  257.7 487.6 %reduce-scatter.14.cloned.1.call-start = ((), (), s32[]{:S(2)}) async-start(), calls=%async_computation.13 | async-start | bytes 9437184 | tf_op jit(solution)/shard_map/reduce_scatter | solution.py:329
  374.9 520.7 %reduce-scatter.12.cloned.1.call-start = ((), (), s32[]{:S(2)}) async-start(), calls=%async_computation.12 | async-start | bytes 9437184 | tf_op jit(solution)/shard_map/reduce_scatter | solution.py:323
  491.5 524.7 %reduce-scatter.8.cloned.1.call-start = ((), (), s32[]{:S(2)}) async-start(), calls=%async_computation.10 | async-start | bytes 7077888 | tf_op jit(solution)/shard_map/reduce_scatter | solution.py:311
  495.2 29.8 %copy-start.19 = (f32[128,16]{0,1:T(8,128)S(1)}, f32[128,16]{0,1:T(8,128)}, u32[]{:S(2)}) copy-start(f32[128,16]{0,1:T(8,128)} %get-tuple-element.54) | copy-start | bytes 24580
  541.9 23.7 %copy-start.25 = (bf16[128]{0:T(256)(128)(2,1)S(1)}, bf16[128]{0:T(256)(128)(2,1)}, u32[]{:S(2)}) copy-start(bf16[128]{0:T(256)(128)(2,1)} %param.27) | copy-start | bytes 772
  541.9 40.2 %copy-start.5 = (bf16[256,4096]{1,0:T(8,128)(2,1)S(1)}, bf16[256,4096]{1,0:T(8,128)(2,1)}, u32[]{:S(2)}) copy-start(bf16[256,4096]{1,0:T(8,128)(2,1)} %copy-done.4) | copy-start | bytes 6291460
  542.0 544.8 %all-reduce.10.cloned.1.call-start = ((), (), s32[]{:S(2)}) async-start(), calls=%async_computation.15 | async-start | bytes 6291456 | tf_op jit(solution)/shard_map/psum | solution.py:339
  595.0 421.3 %copy-start.2 = (bf16[256,3072]{1,0:T(8,128)(2,1)S(1)}, bf16[256,3072]{1,0:T(8,128)(2,1)}, u32[]{:S(2)}) copy-start(bf16[256,3072]{1,0:T(8,128)(2,1)} %convert_element_type.200) | copy-start | bytes 4718596
  1016.2 8.2 copy-start.1
  1022.2 48.2 %copy-start.7 = (bf16[128,2,1024]{2,1,0:T(2,128)(2,1)S(1)}, bf16[128,2,1024]{2,1,0:T(2,128)(2,1)}, u32[]{:S(2)}) copy-start(bf16[128,2,1024]{2,1,0:T(2,128)(2,1)} %param.15) | copy-start | bytes 1572868
  1068.7 26.7 %copy-start.29 = (f32[128]{0:T(128)}, f32[128]{0:T(128)S(1)}, u32[]{:S(2)}) copy-start(f32[128]{0:T(128)S(1)} %convert_element_type.212) | copy-start | bytes 1540
  1086.7 7.1 copy-start.17
  (20 other events, 65.3 us)
Sparse Core Ops, SparseCore 0:
  10.2 101.5 all-gather.11
  143.6 33.1 all-gather.13
  179.0 49.0 all-gather.15
  230.0 123.2 all-gather.17
  355.3 122.6 all-gather.19
  480.3 42.7 reduce-scatter.15
  526.7 68.4 reduce-scatter.9
  598.8 146.5 reduce-scatter.13
  749.0 146.5 reduce-scatter.11
  899.1 117.1 reduce-scatter.7
  1018.8 67.8 all-reduce.9
where the time goes:
time: 1110 us; the launch traced here: 1100 us
  waiting for transfers between devices  729 us (66%)
  blocking collectives  173 us (16%)
  matrix products  87.1 us (8%)
  local copies, waits for them, and re-layouts  65.1 us (6%)
  other arithmetic  31.2 us (3%)
  between operations  16.6 us (1%)
    reduce_scatter x1, waiting for transfers between devices, body(): lax.psum_scatter(terms[6].astype(jnp.bfloat16), 'dp', scatter_dimension=0...  150 us
    reduce_scatter x1, waiting for transfers between devices, body(): lax.psum_scatter(terms[8].astype(jnp.bfloat16), 'dp', scatter_dimension=0...  147 us
    reduce_scatter x1, waiting for transfers between devices, body(): lax.psum_scatter(terms[2].astype(jnp.bfloat16), 'dp', scatter_dimension=0...  121 us
    all_gather x1, waiting for transfers between devices, body(): lax.all_gather(down_weight, 'dp', axis=0, tiled=True)  103 us
    all_gather x1, waiting for transfers between devices, body(): lax.all_gather(up_weight, 'dp', axis=0, tiled=True)  68.7 us
    all_gather x1, waiting for transfers between devices, body(): lax.all_gather(dense_weight, 'dp', axis=0, tiled=True)  40.4 us
    unnamed x1, blocking collectives  35.3 us
    all_gather x1, waiting for transfers between devices, body(): lax.all_gather(attend_weight, 'dp', axis=0, tiled=True)  29.6 us
  transfers between devices with their start and end apart: 11, of which 10 were waited for; matrix products, arithmetic and copies ran while one was open for 12% of the time, Pallas kernels for 0%

commit v1 on v0

--- a/solution.py
+++ b/solution.py
@@ -1,3 +1,4 @@
+import functools
 import math
 import jax
 import jax.numpy as jnp
@@ -11,6 +12,33 @@
 EPSILON = 1e-05
 ROOT_HALF = 0.7071067811865476
 NORMAL_PEAK = 0.3989422804014327
+
+
+def solve_floor_over_axis(point, along_axis):
+    work_now = jax.lax.axis_index(along_axis)
+    block_last = jax.lax.axis_size(along_axis)
+    side_arr, v_now, seen_now = (block_last, work_now, point.shape[0])
+    blocks_here = [d * side_arr if p == 0 else d for p, d in enumerate(point.shape)]
+    k_now = lax.dynamic_update_slice_in_dim(
+        jnp.zeros(blocks_here, point.dtype), point, v_now * seen_now, axis=0
+    )
+    top = z1 = point
+    for m in range(1, side_arr // 2 + 1):
+        top = jax.lax.ppermute(top, along_axis, [(p, (p + 1) % side_arr) for p in range(side_arr)])
+        k_now = lax.dynamic_update_slice_in_dim(
+            k_now, top, (v_now - m) % side_arr * seen_now, axis=0
+        )
+        if 2 * m < side_arr:
+            z1 = jax.lax.ppermute(
+                z1, along_axis, [(p, (p - 1) % side_arr) for p in range(side_arr)]
+            )
+            k_now = lax.dynamic_update_slice_in_dim(
+                k_now, z1, (v_now + m) % side_arr * seen_now, axis=0
+            )
+    return k_now
+
+
+try_all_scenes = functools.partial(solve_floor_over_axis, along_axis="dp")
 
 
 def place_of(block_order, first_slot, count):
@@ -90,7 +118,7 @@
     ) = (
         lax.all_gather(norm_gain, "dp", axis=0, tiled=True),
         lax.all_gather(norm_bias, "dp", axis=0, tiled=True),
-        lax.all_gather(attend_weight, "dp", axis=0, tiled=True),
+        try_all_scenes(attend_weight),
         lax.all_gather(attend_bias, "dp", axis=0, tiled=True),
         lax.all_gather(dense_weight, "dp", axis=0, tiled=True),
         lax.all_gather(dense_bias, "dp", axis=0, tiled=True),

time: 1110 us -> 1200 us (1.081)
  waiting for transfers between devices: 729 us -> 787 us
  blocking collectives: 173 us -> 191 us
  starting transfers between devices: 1.23 us -> 18.2 us
    ppermute x0 -> x7, waiting for transfers between devices: none -> 64.2 us  [the longest x4 62.7 us: solve_floor_over_axis(): jax.lax.ppermute(top, along_axis, [(p, (p + 1) % side_arr) for p in range...]
    all_gather x1 -> x0, waiting for transfers between devices: 29.6 us -> none  [body(): lax.all_gather(attend_weight, 'dp', axis=0, tiled=True)]
    all_gather x1, blocking collectives: 22.8 us -> 41.9 us  [body(): lax.all_gather(norm_gain, 'dp', axis=0, tiled=True)]
    ppermute x0 -> x7, starting transfers between devices: none -> 17.4 us  [the longest x3 10.2 us: solve_floor_over_axis(): jax.lax.ppermute(z1, along_axis, [(p, (p - 1) % side_arr) for p in range(...]
    unnamed x12 -> x11, waiting for transfers between devices: 28.9 us -> 30.5 us
  transfers between devices with their start and end apart: 11 -> 17, of which waited for: 10 -> 15; matrix products, arithmetic and copies ran while one was open for 12% -> 10% of each run, Pallas kernels for 0% -> 0%
where the time goes in v1:
time: 1200 us; the launch traced here: 1190 us
  waiting for transfers between devices  787 us (66%)
  blocking collectives  191 us (16%)
  matrix products  80.7 us (7%)
  local copies, waits for them, and re-layouts  64.7 us (5%)
  other arithmetic  32.7 us (3%)
  starting transfers between devices  18.2 us (2%)
  between operations  17.1 us (1%)
    reduce_scatter x1, waiting for transfers between devices, body(): lax.psum_scatter(terms[8].astype(jnp.bfloat16), 'dp', scatter_dimension=0...  150 us
    reduce_scatter x1, waiting for transfers between devices, body(): lax.psum_scatter(terms[6].astype(jnp.bfloat16), 'dp', scatter_dimension=0...  150 us
    reduce_scatter x1, waiting for transfers between devices, body(): lax.psum_scatter(terms[2].astype(jnp.bfloat16), 'dp', scatter_dimension=0...  121 us
    all_gather x1, waiting for transfers between devices, body(): lax.all_gather(down_weight, 'dp', axis=0, tiled=True)  104 us
    all_gather x1, waiting for transfers between devices, body(): lax.all_gather(up_weight, 'dp', axis=0, tiled=True)  79.1 us
    ppermute x4, waiting for transfers between devices, solve_floor_over_axis(): jax.lax.ppermute(top, along_axis, [(p, (p + 1) % side_arr) for p in range...  62.7 us
    all_gather x1, blocking collectives, body(): lax.all_gather(norm_gain, 'dp', axis=0, tiled=True)  41.9 us
    all_gather x1, waiting for transfers between devices, body(): lax.all_gather(dense_weight, 'dp', axis=0, tiled=True)  40.4 us
  transfers between devices with their start and end apart: 17, of which 15 were waited for; matrix products, arithmetic and copies ran while one was open for 10% of the time, Pallas kernels for 0%

profile of v1, /device:TPU:0, one launch (start us, length us, event | category | flops | bytes accessed | tf_op | source)
XLA Modules:
  0.0 1192.1 jit_solution(2513914126929263583)
XLA Ops:
  17.5 41.9 %all-gather = bf16[8,1,128]{2,1,0:T(2,128)(2,1)S(1)} all-gather(bf16[1,1,128]{2,1,0:T(2,128)(2,1)} %bitcast.110), channel_id=1, replica_groups=mesh['dp'=8,'ctx'=4] {'dp'}, dimensions={0}, use_global_device_ids=true | all-gather | bytes 2304 | tf_op jit(solution)/shard_map/all_gather | solution.py:119
  59.4 16.5 %all-gather.1 = bf16[8,1,128]{2,1,0:T(2,128)(2,1)S(1)} all-gather(bf16[1,1,128]{2,1,0:T(2,128)(2,1)} %bitcast.111), channel_id=1, replica_groups=mesh['dp'=8,'ctx'=4] {'dp'}, dimensions={0}, use_global_device_ids=true | all-gather | bytes 2304 | tf_op jit(solution)/shard_map/all_gather | solution.py:120
  78.7 28.6 %all-gather.2 = bf16[8,1,384]{2,1,0:T(2,128)(2,1)S(1)} all-gather(bf16[1,1,384]{2,1,0:T(2,128)(2,1)S(1)} %reshape.296), channel_id=1, replica_groups=mesh['dp'=8,'ctx'=4] {'dp'}, dimensions={0}, use_global_device_ids=true | all-gather | bytes 6912 | tf_op jit(solution)/shard_map/all_gather | solution.py:122
  114.1 29.3 %collective-permute-done.2 = bf16[128,3072]{1,0:T(8,128)(2,1)S(1)} collective-permute-done((bf16[128,3072]{1,0:T(8,128)(2,1)}, bf16[128,3072]{1,0:T(8,128)(2,1)S(1)}, u32[]{:S(2)}, u32[]{:S(2)}) %collective-permute-start.2) | collective-permute-done | bytes 786464 | tf_op jit(solution)/shard_map/ppermute | solution.py:27
  149.5 22.0 %collective-permute-done.4 = bf16[128,3072]{1,0:T(8,128)(2,1)S(1)} collective-permute-done((bf16[128,3072]{1,0:T(8,128)(2,1)S(1)}, bf16[128,3072]{1,0:T(8,128)(2,1)S(1)}, u32[]{:S(2)}, u32[]{:S(2)}) %collective-permute-start.4) | collective-permute-done | bytes 786464 | tf_op jit(solution)/shard_map/ppermute | solution.py:27
  175.0 11.4 collective-permute-done.6
  219.2 30.2 %all-gather.11.cloned.1.call-done = bf16[512,2,2048]{0,2,1:T(8,128)(2,1)} async-done(((bf16[128,2,2048]{0,2,1:T(8,128)(2,1)}), bf16[512,2,2048]{0,2,1:T(8,128)(2,1)}) %all-gather.11.cloned.1.call-update) | async-done | bytes 4194320 | tf_op jit(solution)/shard_map/all_gather | solution.py:188
  260.2 40.4 %all-gather.13.cloned.1.call-done = bf16[1024,1024]{1,0:T(8,128)(2,1)} async-done(((bf16[128,1024]{1,0:T(8,128)(2,1)}), bf16[1024,1024]{1,0:T(8,128)(2,1)}) %all-gather.13.cloned.1.call-update) | async-done | bytes 2097168 | tf_op jit(solution)/shard_map/all_gather | solution.py:123
  312.6 6.4 copy.60
  333.7 28.7 %reduce-scatter.16.cloned.1.call-done = bf16[128,4096]{1,0:T(8,128)(2,1)} async-done(((bf16[512,4096]{1,0:T(8,128)(2,1)}), bf16[128,4096]{1,0:T(8,128)(2,1)}) %reduce-scatter.16.cloned.1.call-update) | async-done | bytes 1048592
  381.8 28.1 %all-gather.4 = bf16[8,1,512]{2,1,0:T(2,128)(2,1)S(1)} all-gather(bf16[1,1,512]{2,1,0:T(2,128)(2,1)S(1)} %reshape.300), channel_id=1, replica_groups=mesh['dp'=8,'ctx'=4] {'dp'}, dimensions={0}, use_global_device_ids=true | all-gather | bytes 9216 | tf_op jit(solution)/shard_map/all_gather | solution.py:126
  410.0 79.1 %all-gather.15.cloned.1.call-done = bf16[1024,4096]{1,0:T(8,128)(2,1)} async-done(((bf16[128,4096]{1,0:T(8,128)(2,1)}), bf16[1024,4096]{1,0:T(8,128)(2,1)}) %all-gather.15.cloned.1.call-update) | async-done | bytes 8388624 | tf_op jit(solution)/shard_map/all_gather | solution.py:125
  489.1 14.5 %fusion.5 = (bf16[256,4096]{1,0:T(8,128)(2,1)S(1)}, f32[256,4096]{1,0:T(8,128)}) fusion(f32[4096]{0:T(1024)S(1)} %bitcast.106, bf16[256,1024]{1,0:T(8,128)(2,1)S(1)} %copy-done.5, bf16[1024,4096]{1,0:T(8,128)(2,1)} %all-gather.15.cloned.1.call-done), kind=kOutput, calls=%fused_computation.14 | convolution fusion | flops 2216689664 | bytes 15220736 | tf_op jit(solution)/shard_map/dot_general | solution.py:193
  509.4 104.4 %all-gather.17.cloned.1.call-done = bf16[4096,1024]{1,0:T(8,128)(2,1)} async-done(((bf16[512,1024]{1,0:T(8,128)(2,1)}), bf16[4096,1024]{1,0:T(8,128)(2,1)}) %all-gather.17.cloned.1.call-update) | async-done | bytes 8388624 | tf_op jit(solution)/shard_map/all_gather | solution.py:127
  613.8 6.6 fusion.64
  630.5 17.7 %all-gather.3 = bf16[8,1,128]{2,1,0:T(2,128)(2,1)S(1)} all-gather(bf16[1,1,128]{2,1,0:T(2,128)(2,1)S(1)} %bitcast.112), channel_id=1, replica_groups=mesh['dp'=8,'ctx'=4] {'dp'}, dimensions={0}, use_global_device_ids=true | all-gather | bytes 2304 | tf_op jit(solution)/shard_map/all_gather | solution.py:124
  648.2 17.1 %all-gather.5 = bf16[8,1,128]{2,1,0:T(2,128)(2,1)S(1)} all-gather(bf16[1,1,128]{2,1,0:T(2,128)(2,1)S(1)} %bitcast.113), channel_id=1, replica_groups=mesh['dp'=8,'ctx'=4] {'dp'}, dimensions={0}, use_global_device_ids=true | all-gather | bytes 2304 | tf_op jit(solution)/shard_map/all_gather | solution.py:128
  672.5 7.5 fusion.66
  684.4 120.6 %reduce-scatter.8.cloned.1.call-done = bf16[128,3072]{1,0:T(8,128)(2,1)} async-done(((bf16[1024,3072]{1,0:T(8,128)(2,1)}), bf16[128,3072]{1,0:T(8,128)(2,1)}) %reduce-scatter.8.cloned.1.call-update) | async-done | bytes 786448 | tf_op jit(solution)/shard_map/reduce_scatter | solution.py:339
  805.0 150.4 %reduce-scatter.14.cloned.1.call-done = bf16[512,1024]{1,0:T(8,128)(2,1)} async-done(((bf16[4096,1024]{1,0:T(8,128)(2,1)}), bf16[512,1024]{1,0:T(8,128)(2,1)}) %reduce-scatter.14.cloned.1.call-update) | async-done | bytes 1048592 | tf_op jit(solution)/shard_map/reduce_scatter | solution.py:357
  955.5 150.3 %reduce-scatter.12.cloned.1.call-done = bf16[128,4096]{1,0:T(8,128)(2,1)} async-done(((bf16[1024,4096]{1,0:T(8,128)(2,1)}), bf16[128,4096]{1,0:T(8,128)(2,1)}) %reduce-scatter.12.cloned.1.call-update) | async-done | bytes 1048592 | tf_op jit(solution)/shard_map/reduce_scatter | solution.py:351
  1115.8 34.9 %all-reduce.5 = (bf16[1024]{0:T(1024)(128)(2,1)S(1)}, bf16[1024]{0:T(1024)(128)(2,1)S(1)}, bf16[3072]{0:T(1024)(128)(2,1)S(1)}, bf16[1024]{0:T(1024)(128)(2,1)S(1)}, bf16[4096]{0:T(1024)(128)(2,1)S(1)}) all-reduce(bf16[1024]{0:T(1024)(128)(2,1)S(1)} %get-tuple-element.12, ...), channel_id=3, replica_groups=mesh['dp'=8,'ctx'=4] {'dp'}, use_global_device_ids=true, to_apply=%region_10.11.clone | all-reduce | flops 10240 | bytes 40960
  1151.1 6.5 all-reduce.6
  1163.0 12.9 %all-reduce.10.cloned.1.call-done = (bf16[128,3072]{1,0:T(8,128)(2,1)}, bf16[128,1024]{1,0:T(8,128)(2,1)}, bf16[128,4096]{1,0:T(8,128)(2,1)}, bf16[512,1024]{1,0:T(8,128)(2,1)}) async-done(((bf16[128,3072]{1,0:T(8,128)(2,1)}, bf16[128,1024]{1,0:T(8,128)(2,1)}, bf16[128,4096]{1,0:T(8,128)(2,1)}, bf16[512,1024]{1,0:T(8,128)(2,1)}), (bf16[128,3072]{1,0:T(8,128)(2,1)}, bf16[128,1024]{1,0:T(8,128)(2,1)}, ...) | async-done | bytes 3145744 | tf_op jit(solution)/shard_map/psum | solution.py:367
  (204 shorter events, 169.0 us)
Async XLA Ops:
  7.2 242.2 %all-gather.11.cloned.1.call-start = ((), (), s32[]{:S(2)}) async-start(), calls=%async_computation.5 | async-start | bytes 5242880 | tf_op jit(solution)/shard_map/all_gather | solution.py:188
  7.2 103.7 %collective-permute-start.1 = (bf16[128,3072]{1,0:T(8,128)(2,1)}, bf16[128,3072]{1,0:T(8,128)(2,1)S(1)}, u32[]{:S(2)}, u32[]{:S(2)}) collective-permute-start(bf16[128,3072]{1,0:T(8,128)(2,1)} %param.20), channel_id=1, source_target_pairs={{0,28},{4,0},{8,4},{12,8},{16,12},{20,16},{24,20},{28,24},{1,29},{... | collective-permute-start | bytes 2359304 | tf_op jit(solution)/shard_map/ppermute | solution.py:32
  13.3 94.3 %collective-permute-start = (bf16[128,3072]{1,0:T(8,128)(2,1)}, bf16[128,3072]{1,0:T(8,128)(2,1)}, u32[]{:S(2)}, u32[]{:S(2)}) collective-permute-start(bf16[128,3072]{1,0:T(8,128)(2,1)} %param.20), channel_id=1, source_target_pairs={{0,4},{4,8},{8,12},{12,16},{16,20},{20,24},{24,28},{28,0},{1,5},{5... | collective-permute-start | bytes 2359304 | tf_op jit(solution)/shard_map/ppermute | solution.py:27
  75.9 35.0 %copy-start.20 = (bf16[128,3072]{1,0:T(8,128)(2,1)S(1)}, bf16[128,3072]{1,0:T(8,128)(2,1)}, u32[]{:S(2)}) copy-start(bf16[128,3072]{1,0:T(8,128)(2,1)} %param.20) | copy-start | bytes 2359300
  107.6 78.9 %copy-start.4 = (bf16[256,1024]{1,0:T(8,128)(2,1)}, bf16[256,1024]{1,0:T(8,128)(2,1)S(1)}, u32[]{:S(2)}) copy-start(bf16[256,1024]{1,0:T(8,128)(2,1)S(1)} %reshape.282) | copy-start | bytes 1572868
  107.6 35.7 %collective-permute-start.2 = (bf16[128,3072]{1,0:T(8,128)(2,1)}, bf16[128,3072]{1,0:T(8,128)(2,1)S(1)}, u32[]{:S(2)}, u32[]{:S(2)}) collective-permute-start(bf16[128,3072]{1,0:T(8,128)(2,1)} %collective-permute-done), channel_id=1, source_target_pairs={{0,4},{4,8},{8,12},{12,16},{16,20},{20,24},{24,28},{28,0},{1,5},{5... | collective-permute-start | bytes 2359304 | tf_op jit(solution)/shard_map/ppermute | solution.py:27
  111.0 36.8 %collective-permute-start.3 = (bf16[128,3072]{1,0:T(8,128)(2,1)S(1)}, bf16[128,3072]{1,0:T(8,128)(2,1)S(1)}, u32[]{:S(2)}, u32[]{:S(2)}) collective-permute-start(bf16[128,3072]{1,0:T(8,128)(2,1)S(1)} %collective-permute-done.1), channel_id=1, source_target_pairs={{0,28},{4,0},{8,4},{12,8},{16,12},{20,16},{24,20},{28,24},{1,29},{... | collective-permute-start | bytes 2359304 | tf_op jit(solution)/shard_map/ppermute | solution.py:32
  143.3 28.1 %collective-permute-start.4 = (bf16[128,3072]{1,0:T(8,128)(2,1)S(1)}, bf16[128,3072]{1,0:T(8,128)(2,1)S(1)}, u32[]{:S(2)}, u32[]{:S(2)}) collective-permute-start(bf16[128,3072]{1,0:T(8,128)(2,1)S(1)} %collective-permute-done.2), channel_id=1, source_target_pairs={{0,4},{4,8},{8,12},{12,16},{16,20},{20,24},{24,28},{28,0},{1,5},{5... | collective-permute-start | bytes 2359304 | tf_op jit(solution)/shard_map/ppermute | solution.py:27
  147.7 27.1 %collective-permute-start.5 = (bf16[128,3072]{1,0:T(8,128)(2,1)S(1)}, bf16[128,3072]{1,0:T(8,128)(2,1)S(1)}, u32[]{:S(2)}, u32[]{:S(2)}) collective-permute-start(bf16[128,3072]{1,0:T(8,128)(2,1)S(1)} %collective-permute-done.3), channel_id=1, source_target_pairs={{0,28},{4,0},{8,4},{12,8},{16,12},{20,16},{24,20},{28,24},{1,29},{... | collective-permute-start | bytes 2359304 | tf_op jit(solution)/shard_map/ppermute | solution.py:32
  171.5 14.9 %collective-permute-start.6 = (bf16[128,3072]{1,0:T(8,128)(2,1)S(1)}, bf16[128,3072]{1,0:T(8,128)(2,1)S(1)}, u32[]{:S(2)}, u32[]{:S(2)}) collective-permute-start(bf16[128,3072]{1,0:T(8,128)(2,1)S(1)} %collective-permute-done.4), channel_id=1, source_target_pairs={{0,4},{4,8},{8,12},{12,16},{16,20},{20,24},{24,28},{28,0},{1,5},{5... | collective-permute-start | bytes 2359304 | tf_op jit(solution)/shard_map/ppermute | solution.py:27
  215.5 85.1 %all-gather.13.cloned.1.call-start = ((), (), s32[]{:S(2)}) async-start(), calls=%async_computation.6 | async-start | bytes 2359296 | tf_op jit(solution)/shard_map/all_gather | solution.py:123
  216.2 146.1 %reduce-scatter.16.cloned.1.call-start = ((), (), s32[]{:S(2)}) async-start(), calls=%async_computation.13 | async-start | bytes 5242880
  219.2 32.7 %copy-start.18 = (bf16[128,2,16,48]{0,3,2,1:T(8,128)(2,1)S(1)}, bf16[128,2,16,48]{0,3,2,1:T(8,128)(2,1)}, u32[]{:S(2)}) copy-start(bf16[128,2,16,48]{0,3,2,1:T(8,128)(2,1)} %slice.155) | copy-start | bytes 1179652
  257.4 43.2 %copy-start.12 = (bf16[128,2,1024]{2,1,0:T(2,128)(2,1)S(1)}, bf16[128,2,1024]{2,1,0:T(2,128)(2,1)}, u32[]{:S(2)}) copy-start(bf16[128,2,1024]{2,1,0:T(2,128)(2,1)} %get-tuple-element.31) | copy-start | bytes 1572868
  319.1 170.1 %all-gather.15.cloned.1.call-start = ((), (), s32[]{:S(2)}) async-start(), calls=%async_computation.7 | async-start | bytes 9437184 | tf_op jit(solution)/shard_map/all_gather | solution.py:125
  319.6 294.1 %all-gather.17.cloned.1.call-start = ((), (), s32[]{:S(2)}) async-start(), calls=%async_computation.8 | async-start | bytes 9437184 | tf_op jit(solution)/shard_map/all_gather | solution.py:127
  320.2 364.2 %reduce-scatter.10.cloned.1.call-start = ((), (), s32[]{:S(2)}) async-start(), calls=%async_computation.10 | async-start | bytes 2359296 | tf_op jit(solution)/shard_map/reduce_scatter | solution.py:345
  328.3 476.8 %reduce-scatter.8.cloned.1.call-start = ((), (), s32[]{:S(2)}) async-start(), calls=%async_computation.9 | async-start | bytes 7077888 | tf_op jit(solution)/shard_map/reduce_scatter | solution.py:339
  381.1 108.0 %copy-start.5 = (bf16[256,1024]{1,0:T(8,128)(2,1)S(1)}, bf16[256,1024]{1,0:T(8,128)(2,1)}, u32[]{:S(2)}) copy-start(bf16[256,1024]{1,0:T(8,128)(2,1)} %copy-done.4) | copy-start | bytes 1572868
  381.2 574.3 %reduce-scatter.14.cloned.1.call-start = ((), (), s32[]{:S(2)}) async-start(), calls=%async_computation.12 | async-start | bytes 9437184 | tf_op jit(solution)/shard_map/reduce_scatter | solution.py:357
  509.4 596.4 %reduce-scatter.12.cloned.1.call-start = ((), (), s32[]{:S(2)}) async-start(), calls=%async_computation.11 | async-start | bytes 9437184 | tf_op jit(solution)/shard_map/reduce_scatter | solution.py:351
  627.3 548.6 %all-reduce.10.cloned.1.call-start = ((), (), s32[]{:S(2)}) async-start(), calls=%async_computation.14 | async-start | bytes 6291456 | tf_op jit(solution)/shard_map/psum | solution.py:367
  672.5 433.2 %copy-start.3 = (bf16[256,3072]{1,0:T(8,128)(2,1)S(1)}, bf16[256,3072]{1,0:T(8,128)(2,1)}, u32[]{:S(2)}) copy-start(bf16[256,3072]{1,0:T(8,128)(2,1)} %convert_element_type.200) | copy-start | bytes 4718596
  1111.7 48.0 %copy-start.9 = (bf16[128,2,1024]{2,1,0:T(2,128)(2,1)S(1)}, bf16[128,2,1024]{2,1,0:T(2,128)(2,1)}, u32[]{:S(2)}) copy-start(bf16[128,2,1024]{2,1,0:T(2,128)(2,1)} %param.15) | copy-start | bytes 1572868
  (26 other events, 176.5 us)
Sparse Core Ops, SparseCore 0:
  215.6 33.7 all-gather.10
  251.5 49.0 all-gather.12
  319.2 43.1 reduce-scatter.15
  364.3 124.7 all-gather.14
  491.1 122.6 all-gather.16
  617.7 66.6 reduce-scatter.9
  688.0 117.0 reduce-scatter.7
  808.7 146.7 reduce-scatter.13
  959.1 146.5 reduce-scatter.11
  1108.2 67.7 all-reduce.9
